TPU v7x, 32 devices: a whole 2x2x4 slice. The times are simulated.
32 devices in a mesh: wide: 8 (over z, x), narrow: 4 (over y, core).
Axes of the slice: x: 2, y: 2, z: 4, core: 2. Of those that a mesh axis runs over, the one named last changes fastest.
Arguments:
- embeddings: bfloat16 [16384, 1024], P(('wide', 'narrow')), may hold values from -32 to 32
- valid: int32 [16384], P(('wide', 'narrow')), may hold values from 0 to 1, as said below
Outputs:
- whitened: bfloat16 [16384, 1024], P(('wide', 'narrow'))
Inputs may be any that keep to these rules, and one draw needn't show every extreme that they name: The first row of every aligned block of 16 rows has valid = 1.
All inputs are finite; a program needn't handle non-finite values.
Results may differ from a plain program's by a relative error of at most 0.001.
Values sent between devices are 32-bit elements; how exact they have to be, the bound alone decides.
No kernel may reach another device: no remote copies, remote signals or barrier semaphores. Data moves between devices by JAX's collectives and lax.ppermute only.
A program may use at most 64 MiB of HBM per device.

v0:
```python
import jax
import jax.numpy as jnp
from jax import lax
from jax.sharding import PartitionSpec as P


def shifted_scatter(gram, count_local, sums_local, center):
    return (
        gram
        - sums_local[:, None] * center[None, :]
        - center[:, None] * sums_local[None, :]
        + count_local * center[:, None] * center[None, :]
    )


def narrow_rows(term):
    return lax.psum_scatter(term, "narrow", scatter_dimension=0, tiled=True)


def on_device(embeddings, valid):
    width = embeddings.shape[1]
    narrow_count = lax.axis_size("narrow")
    row_span = width // narrow_count
    offset = lax.axis_index("narrow") * row_span
    mask_half = valid.astype(jnp.bfloat16)
    count_local = jnp.sum(valid.astype(jnp.float32))
    masked = embeddings * mask_half[:, None]
    gram = lax.dot_general(
        masked, embeddings, (((0,), (0,)), ((), ())), preferred_element_type=jnp.float32
    )
    sums_local = jnp.dot(mask_half[None, :], embeddings, preferred_element_type=jnp.float32)[0]
    count, sums = lax.psum((count_local, sums_local), ("wide", "narrow"))
    term = shifted_scatter(gram, count_local, sums_local, sums / count)
    level_rows = narrow_rows(term)
    own_rows = lax.psum(level_rows, "wide")
    center = sums / count
    cov_rows = own_rows / count
    ident_rows = (
        lax.broadcasted_iota(jnp.int32, (row_span, width), 0) + offset
        == lax.broadcasted_iota(jnp.int32, (row_span, width), 1)
    ).astype(jnp.float32)
    diag_block = lax.dynamic_slice_in_dim(cov_rows, offset, row_span, 1)
    trace_part = jnp.sum(jnp.diagonal(diag_block))
    square_part = jnp.sum(cov_rows * cov_rows)
    trace_cov, square_sum = lax.psum((trace_part, square_part), "narrow")
    ridge_add = 0.05 * trace_cov / width + 1e-06
    norm_frob = jnp.sqrt(square_sum + 2.0 * ridge_add * trace_cov + width * ridge_add * ridge_add)
    base_rows = (cov_rows + ridge_add * ident_rows) / norm_frob
    root_rows = (3.0 * ident_rows - base_rows) / 2.0
    root_full = lax.all_gather(root_rows, "narrow", axis=0, tiled=True)
    first = jnp.dot(
        base_rows, root_full, precision=lax.Precision.HIGHEST, preferred_element_type=jnp.float32
    )
    second = jnp.dot(
        first, root_full, precision=lax.Precision.HIGHEST, preferred_element_type=jnp.float32
    )
    factor = (3.0 * ident_rows - second) / 2.0
    root_rows = jnp.dot(
        factor, root_full, precision=lax.Precision.HIGHEST, preferred_element_type=jnp.float32
    )
    centered_x = embeddings.astype(jnp.float32) - center
    product = jnp.dot(
        centered_x,
        lax.all_gather(root_rows, "narrow", axis=0, tiled=True),
        precision=lax.Precision.HIGHEST,
        preferred_element_type=jnp.float32,
    )
    return (product / jnp.sqrt(norm_frob)).astype(jnp.bfloat16)


def solution(mesh):
    in_specs = (P(("wide", "narrow"), None), P(("wide", "narrow")))
    out_specs = P(("wide", "narrow"), None)
    return jax.shard_map(
        on_device, mesh=mesh, in_specs=in_specs, out_specs=out_specs, check_vma=False
    )
```

profile of v0, /device:TPU:0, one launch (start us, length us, event | category | flops | bytes accessed | tf_op | source)
XLA Modules:
  0.0 300.6 jit_solution(4755402428084836865)
XLA Ops:
  6.5 0.0 reduce-scatter.2.cloned.1.call-start
  6.5 0.7 convert_element_type.14
  7.2 1.3 convert_reduce_fusion
  8.5 1.5 fusion.11
  10.0 42.1 %all-reduce = (f32[1024]{0:T(1024)S(1)}, f32[]{:T(128)}) all-reduce(f32[1024]{0:T(1024)S(1)} %bitcast.12, f32[]{:T(128)} %convert_reduce_fusion), channel_id=1, replica_groups=mesh['wide'=8,'narrow'=4] {'wide','narrow'}, use_global_device_ids=true, to_apply=%region_0.0 | all-reduce | flops 1025 | bytes 8200 | tf_op jit(solution)/shard_map/psum | solution.py:32
  52.1 1.3 broadcast_multiply_fusion
  53.4 5.3 %multiply_add_fusion = f32[1024,1024]{1,0:T(8,128)} fusion(bf16[512,1024]{1,0:T(8,128)(2,1)} %param.2, f32[1024]{0:T(1024)S(1)} %get-tuple-element.11, f32[1024]{0:T(1024)S(1)} %bitcast.13, f32[1024]{0:T(1024)S(1)} %get-tuple-element.12, bf16[512]{0:T(512)(128)(2,1)S(1)} %convert_element_type.14), kind=kOutput, calls=%fused_computation.1 | convolution fusion | flops 1080557568 | bytes 5256192 | tf_op jit(solution)/shard_map/dot_general | solution.py:28
  58.7 0.0 reduce-scatter.2.cloned.1.call-update
  58.7 0.0 all-reduce.4.cloned.1.call-start
  58.8 44.7 %reduce-scatter.2.cloned.1.call-done = f32[256,1024]{1,0:T(8,128)} async-done(((f32[1024,1024]{1,0:T(8,128)}), f32[256,1024]{1,0:T(8,128)}) %reduce-scatter.2.cloned.1.call-update) | async-done | bytes 1048592 | tf_op jit(solution)/shard_map/reduce_scatter | solution.py:17
  103.5 0.0 all-reduce.4.cloned.1.call-update
  103.5 0.0 all-gather.3.cloned.1.call-start
  103.6 81.6 %all-reduce.4.cloned.1.call-done = f32[256,1024]{1,0:T(8,128)} async-done(((f32[256,1024]{1,0:T(8,128)}), f32[256,1024]{1,0:T(8,128)}) %all-reduce.4.cloned.1.call-update) | async-done | bytes 1048592 | tf_op jit(solution)/shard_map/psum | solution.py:35
  185.2 2.7 multiply_reduce_fusion
  188.0 2.3 gather_fusion
  190.4 0.7 reduce_sum.28
  191.0 7.2 %all-reduce.1 = (f32[]{:T(128)}, f32[]{:T(128)}) all-reduce(f32[]{:T(128)} %get-tuple-element.9, f32[]{:T(128)} %reduce_sum.28), channel_id=1, replica_groups=mesh['wide'=8,'narrow'=4] {'narrow'}, use_global_device_ids=true, to_apply=%region_8.9 | all-reduce | flops 2 | bytes 16 | tf_op jit(solution)/shard_map/psum | solution.py:45
  200.3 1.3 fusion.7
  201.6 0.0 all-gather.3.cloned.1.call-update
  201.6 0.2 all-gather.5.cloned.1.call-start
  201.8 33.4 %all-gather.3.cloned.1.call-done = f32[1024,1024]{1,0:T(8,128)} async-done(((f32[256,1024]{1,0:T(8,128)}), f32[1024,1024]{1,0:T(8,128)}) %all-gather.3.cloned.1.call-update) | async-done | bytes 4194320 | tf_op jit(solution)/shard_map/all_gather | solution.py:50
  235.2 0.0 copy-start
  235.2 6.1 %fusion.10 = f32[256,1024]{1,0:T(8,128)S(1)} fusion(f32[1024,1024]{1,0:T(8,128)} %all-gather.3.cloned.1.call-done, f32[256,1024]{1,0:T(8,128)S(1)} %get-tuple-element.10, f32[]{:T(128)S(6)} %sqrt.6, f32[]{:T(128)S(6)} %add.45, s32[256]{0:T(256)S(1)} %iota_add_fusion), kind=kOutput, calls=%fused_computation.23 | convolution fusion | flops 3222274048 | bytes 6292488 | tf_op jit(solution)/shard_map/dot_general | solution.py:51
  241.4 0.0 copy-done
  241.4 3.7 %fusion.4 = f32[256,1024]{1,0:T(8,128)S(1)} fusion(f32[256,1024]{1,0:T(8,128)S(1)} %fusion.10, f32[1024,1024]{1,0:T(8,128)S(1)} %copy-done, s32[256]{0:T(256)S(1)} %iota_add_fusion), kind=kOutput, calls=%fused_computation.9 | convolution fusion | flops 3222274048 | bytes 6292480 | tf_op jit(solution)/shard_map/dot_general | solution.py:54
  245.1 0.0 copy-start.1
  245.2 4.7 %fusion.12 = f32[256,1024]{1,0:T(8,128)} fusion(f32[256,1024]{1,0:T(8,128)S(1)} %fusion.4, f32[1024,1024]{1,0:T(8,128)S(1)} %copy-done), kind=kOutput, calls=%fused_computation.25 | convolution fusion | flops 3221225472 | bytes 6291456 | tf_op jit(solution)/shard_map/dot_general | solution.py:58
  249.8 0.0 all-gather.5.cloned.1.call-update
  249.9 34.6 %all-gather.5.cloned.1.call-done = f32[1024,1024]{1,0:T(8,128)} async-done(((f32[256,1024]{1,0:T(8,128)}), f32[1024,1024]{1,0:T(8,128)}) %all-gather.5.cloned.1.call-update) | async-done | bytes 4194320 | tf_op jit(solution)/shard_map/all_gather | solution.py:64
  284.5 0.0 copy-done.1
  284.5 9.6 %divide_convert_fusion = bf16[512,1024]{1,0:T(8,128)(2,1)} fusion(f32[1024,1024]{1,0:T(8,128)} %all-gather.5.cloned.1.call-done, bf16[512,1024]{1,0:T(8,128)(2,1)S(1)} %copy-done.1, f32[]{:T(128)S(6)} %sqrt.7, f32[1024]{0:T(1024)S(1)} %get-tuple-element.12), kind=kOutput, calls=%fused_computation.2 | convolution fusion | flops 6444548096 | bytes 6295556 | tf_op jit(solution)/shard_map/dot_general | solution.py:62
  (4 shorter events, 0.0 us)
Async XLA Ops:
  6.5 97.0 %reduce-scatter.2.cloned.1.call-start = ((), (), s32[]{:S(2)}) async-start(), calls=%async_computation.1 | async-start | bytes 5242880 | tf_op jit(solution)/shard_map/reduce_scatter | solution.py:17
  58.7 126.5 %all-reduce.4.cloned.1.call-start = ((), (), s32[]{:S(2)}) async-start(), calls=%async_computation.2 | async-start | bytes 2097152 | tf_op jit(solution)/shard_map/psum | solution.py:35
  103.5 131.7 %all-gather.3.cloned.1.call-start = ((), (), s32[]{:S(2)}) async-start(), calls=%async_computation.3 | async-start | bytes 5242880 | tf_op jit(solution)/shard_map/all_gather | solution.py:50
  201.6 82.9 %all-gather.5.cloned.1.call-start = ((), (), s32[]{:S(2)}) async-start(), calls=%async_computation.4 | async-start | bytes 5242880 | tf_op jit(solution)/shard_map/all_gather | solution.py:64
  235.2 6.1 %copy-start = (f32[1024,1024]{1,0:T(8,128)S(1)}, f32[1024,1024]{1,0:T(8,128)}, u32[]{:S(2)}) copy-start(f32[1024,1024]{1,0:T(8,128)} %all-gather.3.cloned.1.call-done) | copy-start | bytes 12582916
  245.1 39.3 %copy-start.1 = (bf16[512,1024]{1,0:T(8,128)(2,1)S(1)}, bf16[512,1024]{1,0:T(8,128)(2,1)}, u32[]{:S(2)}) copy-start(bf16[512,1024]{1,0:T(8,128)(2,1)} %param.2) | copy-start | bytes 3145732
Sparse Core Ops, SparseCore 0:
  58.9 44.6 reduce-scatter.1
  107.0 78.1 all-reduce.3
  201.7 33.4 all-gather.2
  250.0 34.4 all-gather.4
where the time goes:
time: 301 us
  waiting for transfers between devices  194 us (64%)
  blocking collectives  49.3 us (16%)
  matrix products  30.9 us (10%)
  between operations  15.3 us (5%)
  other arithmetic  7.97 us (3%)
    psum x1, waiting for transfers between devices, on_device(): own_rows = lax.psum(level_rows, 'wide')  81.6 us
    reduce_scatter x1, waiting for transfers between devices, narrow_rows(): return lax.psum_scatter(term, 'narrow', scatter_dimension=0, tiled=True)  44.7 us
    psum x1, blocking collectives, on_device(): count, sums = lax.psum((count_local, sums_local), ('wide', 'narrow'))  42.1 us
    all_gather x1, waiting for transfers between devices, on_device(): lax.all_gather(root_rows, 'narrow', axis=0, tiled=True)  34.6 us
    all_gather x1, waiting for transfers between devices, on_device(): root_full = lax.all_gather(root_rows, 'narrow', axis=0, tiled=True)  33.4 us
    dot_general x1, matrix products, on_device(): jnp.dot(centered_x, lax.all_gather(root_rows, 'narrow', axis=0, tiled=Tru...  9.62 us
    psum x1, blocking collectives, on_device(): trace_cov, square_sum = lax.psum((trace_part, square_part), 'narrow')  7.19 us
    dot_general x1, matrix products, on_device(): jnp.dot(base_rows, root_full, precision=lax.Precision.HIGHEST, preferred_...  6.13 us
  transfers between devices with their start and end apart: 4, of which 4 were waited for; matrix products, arithmetic and copies ran while one was open for 0% of the time, Pallas kernels for 0%

commit v1 on v0

--- a/solution.py
+++ b/solution.py
@@ -32,7 +32,8 @@
     count, sums = lax.psum((count_local, sums_local), ("wide", "narrow"))
     term = shifted_scatter(gram, count_local, sums_local, sums / count)
     level_rows = narrow_rows(term)
-    own_rows = lax.psum(level_rows, "wide")
+    parts = lax.all_gather(level_rows, "wide", axis=0, tiled=False)
+    own_rows = parts.sum(axis=0)
     center = sums / count
     cov_rows = own_rows / count
     ident_rows = (

time: 301 us -> 348 us (1.16)
  waiting for transfers between devices: 194 us -> 239 us
    all_gather x0 -> x1, waiting for transfers between devices: none -> 127 us  [on_device(): parts = lax.all_gather(level_rows, 'wide', axis=0, tiled=False)]
    psum x1 -> x0, waiting for transfers between devices: 81.6 us -> none  [on_device(): own_rows = lax.psum(level_rows, 'wide')]
    reduce_sum x0 -> x1, other arithmetic: none -> 4.42 us  [on_device(): own_rows = parts.sum(axis=0)]
where the time goes in v1:
time: 348 us; the launch traced here: 347 us
  waiting for transfers between devices  239 us (69%)
  blocking collectives  48.7 us (14%)
  matrix products  31 us (9%)
  between operations  15.3 us (4%)
  other arithmetic  11.1 us (3%)
    all_gather x1, waiting for transfers between devices, on_device(): parts = lax.all_gather(level_rows, 'wide', axis=0, tiled=False)  127 us
    reduce_scatter x1, waiting for transfers between devices, narrow_rows(): return lax.psum_scatter(term, 'narrow', scatter_dimension=0, tiled=True)  44.8 us
    psum x1, blocking collectives, on_device(): count, sums = lax.psum((count_local, sums_local), ('wide', 'narrow'))  42.1 us
    all_gather x1, waiting for transfers between devices, on_device(): lax.all_gather(root_rows, 'narrow', axis=0, tiled=True)  34.6 us
    all_gather x1, waiting for transfers between devices, on_device(): root_full = lax.all_gather(root_rows, 'narrow', axis=0, tiled=True)  32.6 us
    dot_general x1, matrix products, on_device(): jnp.dot(centered_x, lax.all_gather(root_rows, 'narrow', axis=0, tiled=Tru...  9.62 us
  transfers between devices with their start and end apart: 4, of which 4 were waited for; matrix products, arithmetic and copies ran while one was open for 0% of the time, Pallas kernels for 0%

profile of v1, /device:TPU:0, one launch (start us, length us, event | category | flops | bytes accessed | tf_op | source)
XLA Modules:
  0.0 347.3 jit_solution(6919717005734200443)
XLA Ops:
  6.5 0.0 reduce-scatter.2.cloned.1.call-start
  6.5 0.7 convert_element_type.14
  7.2 1.3 convert_reduce_fusion
  8.5 1.5 fusion.11
  10.0 42.1 %all-reduce = (f32[1024]{0:T(1024)S(1)}, f32[]{:T(128)}) all-reduce(f32[1024]{0:T(1024)S(1)} %bitcast.14, f32[]{:T(128)} %convert_reduce_fusion), channel_id=1, replica_groups=mesh['wide'=8,'narrow'=4] {'wide','narrow'}, use_global_device_ids=true, to_apply=%region_0.0 | all-reduce | flops 1025 | bytes 8200 | tf_op jit(solution)/shard_map/psum | solution.py:32
  52.1 1.3 broadcast_multiply_fusion
  53.4 5.3 %multiply_add_fusion = f32[1024,1024]{1,0:T(8,128)} fusion(bf16[512,1024]{1,0:T(8,128)(2,1)} %param.2, f32[1024]{0:T(1024)S(1)} %get-tuple-element.11, f32[1024]{0:T(1024)S(1)} %bitcast.15, f32[1024]{0:T(1024)S(1)} %get-tuple-element.12, bf16[512]{0:T(512)(128)(2,1)S(1)} %convert_element_type.14), kind=kOutput, calls=%fused_computation.1 | convolution fusion | flops 1080557568 | bytes 5256192 | tf_op jit(solution)/shard_map/dot_general | solution.py:28
  58.7 0.0 reduce-scatter.2.cloned.1.call-update
  58.7 0.0 all-gather.9.cloned.1.call-start
  58.8 44.8 %reduce-scatter.2.cloned.1.call-done = f32[256,1024]{1,0:T(8,128)} async-done(((f32[1024,1024]{1,0:T(8,128)}), f32[256,1024]{1,0:T(8,128)}) %reduce-scatter.2.cloned.1.call-update) | async-done | bytes 1048592 | tf_op jit(solution)/shard_map/reduce_scatter | solution.py:17
  103.6 0.0 all-gather.9.cloned.1.call-update
  103.6 0.0 all-gather.5.cloned.1.call-start
  103.7 126.5 %all-gather.9.cloned.1.call-done = f32[2048,1024]{1,0:T(8,128)} async-done(((f32[256,1024]{1,0:T(8,128)}), f32[2048,1024]{1,0:T(8,128)}) %all-gather.9.cloned.1.call-update) | async-done | bytes 8388624 | tf_op jit(solution)/shard_map/all_gather | solution.py:35
  230.2 4.4 %reduce_sum.37 = f32[256,1024]{1,0:T(8,128)S(1)} reduce(f32[8,256,1024]{2,1,0:T(8,128)} %bitcast.13, f32[]{:T(128)} %constant.11.clone.1), dimensions={0}, to_apply=%region_4.0 | reduce | flops 1835008 | bytes 9437188 | tf_op jit(solution)/shard_map/reduce_sum | solution.py:36
  234.6 1.5 multiply_reduce_fusion
  236.1 2.3 gather_fusion
  238.5 0.7 reduce_sum.38
  239.2 6.5 %all-reduce.1 = (f32[]{:T(128)}, f32[]{:T(128)}) all-reduce(f32[]{:T(128)} %get-tuple-element.9, f32[]{:T(128)} %reduce_sum.38), channel_id=1, replica_groups=mesh['wide'=8,'narrow'=4] {'narrow'}, use_global_device_ids=true, to_apply=%region_8.9 | all-reduce | flops 2 | bytes 16 | tf_op jit(solution)/shard_map/psum | solution.py:46
  247.8 1.3 fusion.7
  249.1 0.0 all-gather.5.cloned.1.call-update
  249.1 0.2 all-gather.7.cloned.1.call-start
  249.3 32.6 %all-gather.5.cloned.1.call-done = f32[1024,1024]{1,0:T(8,128)} async-done(((f32[256,1024]{1,0:T(8,128)}), f32[1024,1024]{1,0:T(8,128)}) %all-gather.5.cloned.1.call-update) | async-done | bytes 4194320 | tf_op jit(solution)/shard_map/all_gather | solution.py:51
  281.9 0.0 copy-start
  281.9 6.1 %fusion.10 = f32[256,1024]{1,0:T(8,128)S(1)} fusion(f32[1024,1024]{1,0:T(8,128)} %all-gather.5.cloned.1.call-done, f32[256,1024]{1,0:T(8,128)S(1)} %get-tuple-element.10, f32[]{:T(128)S(6)} %sqrt.6, f32[]{:T(128)S(6)} %add.43, s32[256]{0:T(256)S(1)} %iota_add_fusion), kind=kOutput, calls=%fused_computation.23 | convolution fusion | flops 3222274048 | bytes 6292488 | tf_op jit(solution)/shard_map/dot_general | solution.py:52
  288.1 0.0 copy-done
  288.1 3.7 %fusion.4 = f32[256,1024]{1,0:T(8,128)S(1)} fusion(f32[256,1024]{1,0:T(8,128)S(1)} %fusion.10, f32[1024,1024]{1,0:T(8,128)S(1)} %copy-done, s32[256]{0:T(256)S(1)} %iota_add_fusion), kind=kOutput, calls=%fused_computation.9 | convolution fusion | flops 3222274048 | bytes 6292480 | tf_op jit(solution)/shard_map/dot_general | solution.py:55
  291.9 0.0 copy-start.1
  291.9 4.7 %fusion.12 = f32[256,1024]{1,0:T(8,128)} fusion(f32[256,1024]{1,0:T(8,128)S(1)} %fusion.4, f32[1024,1024]{1,0:T(8,128)S(1)} %copy-done), kind=kOutput, calls=%fused_computation.25 | convolution fusion | flops 3221225472 | bytes 6291456 | tf_op jit(solution)/shard_map/dot_general | solution.py:59
  296.5 0.0 all-gather.7.cloned.1.call-update
  296.6 34.6 %all-gather.7.cloned.1.call-done = f32[1024,1024]{1,0:T(8,128)} async-done(((f32[256,1024]{1,0:T(8,128)}), f32[1024,1024]{1,0:T(8,128)}) %all-gather.7.cloned.1.call-update) | async-done | bytes 4194320 | tf_op jit(solution)/shard_map/all_gather | solution.py:65
  331.2 0.0 copy-done.1
  331.2 9.6 %divide_convert_fusion = bf16[512,1024]{1,0:T(8,128)(2,1)} fusion(f32[1024,1024]{1,0:T(8,128)} %all-gather.7.cloned.1.call-done, bf16[512,1024]{1,0:T(8,128)(2,1)S(1)} %copy-done.1, f32[]{:T(128)S(6)} %sqrt.7, f32[1024]{0:T(1024)S(1)} %get-tuple-element.12), kind=kOutput, calls=%fused_computation.2 | convolution fusion | flops 6444548096 | bytes 6295556 | tf_op jit(solution)/shard_map/dot_general | solution.py:63
  (4 shorter events, 0.0 us)
Async XLA Ops:
  6.5 97.0 %reduce-scatter.2.cloned.1.call-start = ((), (), s32[]{:S(2)}) async-start(), calls=%async_computation.1 | async-start | bytes 5242880 | tf_op jit(solution)/shard_map/reduce_scatter | solution.py:17
  58.7 171.4 %all-gather.9.cloned.1.call-start = ((), (), s32[]{:S(2)}) async-start(), calls=%async_computation.4 | async-start | bytes 9437184 | tf_op jit(solution)/shard_map/all_gather | solution.py:35
  103.6 178.4 %all-gather.5.cloned.1.call-start = ((), (), s32[]{:S(2)}) async-start(), calls=%async_computation.2 | async-start | bytes 5242880 | tf_op jit(solution)/shard_map/all_gather | solution.py:51
  249.1 82.1 %all-gather.7.cloned.1.call-start = ((), (), s32[]{:S(2)}) async-start(), calls=%async_computation.3 | async-start | bytes 5242880 | tf_op jit(solution)/shard_map/all_gather | solution.py:65
  281.9 6.1 %copy-start = (f32[1024,1024]{1,0:T(8,128)S(1)}, f32[1024,1024]{1,0:T(8,128)}, u32[]{:S(2)}) copy-start(f32[1024,1024]{1,0:T(8,128)} %all-gather.5.cloned.1.call-done) | copy-start | bytes 12582916
  291.9 39.3 %copy-start.1 = (bf16[512,1024]{1,0:T(8,128)(2,1)S(1)}, bf16[512,1024]{1,0:T(8,128)(2,1)}, u32[]{:S(2)}) copy-start(bf16[512,1024]{1,0:T(8,128)(2,1)} %param.2) | copy-start | bytes 3145732
Sparse Core Ops, SparseCore 0:
  58.9 44.6 reduce-scatter.1
  105.7 124.4 all-gather.8
  249.2 32.6 all-gather.4
  296.7 34.4 all-gather.6
